TPU v7x, 512 devices: a whole 4x8x8 slice. The times are simulated.
512 devices in a mesh: dev: 32 (over y_hi, z), ha: 2 (over y_lo), col: 8 (over x, core).
Axes of the slice: x: 4, y: 8 (y_hi: 4, y_lo: 2; y = y_hi * 2 + y_lo), z: 8, core: 2. Of those that a mesh axis runs over, the one named last changes fastest.
Arguments:
- features: bfloat16 [128, 128, 32, 128], P('col', 'dev', 'ha'), may hold values from -6 to 6
- kernel: bfloat16 [3, 3, 3, 128, 128], P(None, None, None, 'col'), may hold values from -0.109375 to 0.109375
- channel_bias: float32 [128], P('col'), may hold values from -3 to 3
Outputs:
- activated: bfloat16 [128, 128, 32, 128], P('col', 'dev', 'ha')
All inputs are finite; a program needn't handle non-finite values.
Results may differ from a plain program's by a relative error of at most 0.005.
Values may be sent and summed in bfloat16 or wider, within the bound.
A program may use at most 64 MiB of HBM per device.

v0:
```python
import jax
import jax.numpy as jnp
from jax import lax
from jax.sharding import PartitionSpec as P


def with_halo(x, sides, width):
    for axis, dim in sides:
        devices, length = (lax.axis_size(axis), x.shape[dim])
        up = [(i, (i + 1) % devices) for i in range(devices - 1)]
        down = [(j, i) for i, j in up]
        last = lax.slice_in_dim(x, length - width, length, axis=dim)
        first = lax.slice_in_dim(x, 0, width, axis=dim)
        before = lax.ppermute(last, axis, up)
        after = lax.ppermute(first, axis, down)
        x = jnp.concatenate([before, x, after], axis=dim)
    return x


def convolve(padded, weights):
    depth_pad = padded.shape[1]
    height_pad = padded.shape[2]
    width_cells = padded.shape[3]
    outer = weights.shape[3]
    depth_cells = depth_pad - 2
    height_cells = height_pad - 2
    partial_sums = [
        jnp.zeros((outer, depth_cells, height_cells, width_cells), jnp.float32)
        for col_tap in range(3)
    ]
    for depth_tap in range(3):
        planes = padded[:, depth_tap : depth_tap + depth_cells]
        tap_out = lax.dot_general(
            weights[depth_tap], planes, (((3,), (0,)), ((), ())), preferred_element_type=jnp.float32
        )
        for row_tap in range(3):
            for col_tap in range(3):
                partial_sums[col_tap] = (
                    partial_sums[col_tap]
                    + tap_out[row_tap, col_tap, :, :, row_tap : row_tap + height_cells, :]
                )
    zero_column = jnp.zeros((outer, depth_cells, height_cells, 1), jnp.float32)
    from_left = jnp.concatenate([zero_column, partial_sums[0][..., :-1]], axis=3)
    from_right = jnp.concatenate([partial_sums[2][..., 1:], zero_column], axis=3)
    return partial_sums[1] + from_left + from_right


def finish(summed, offsets):
    summed = summed + offsets[:, None, None, None]
    return jnp.where(summed >= 0, summed, 0.3 * summed).astype(jnp.bfloat16)


def per_device(features, kernel, channel_bias):
    padded = with_halo(features, (("dev", 1), ("ha", 2)), 1)
    gathered = lax.all_gather(padded, "col", axis=0, tiled=True)
    return finish(convolve(gathered, kernel), channel_bias)


def solution(mesh):
    in_specs = (P("col", "dev", "ha", None), P(None, None, None, "col", None), P("col"))
    out_specs = P("col", "dev", "ha", None)
    return jax.shard_map(
        per_device, mesh=mesh, in_specs=in_specs, out_specs=out_specs, check_vma=False
    )
```

profile of v0, /device:TPU:1, one launch (start us, length us, event | category | flops | bytes accessed | tf_op | source)
XLA Modules:
  0.0 85.2 jit_solution(9481461446292273636)
XLA Ops:
  6.5 0.0 all-gather.2.cloned.1.call-start
  6.5 0.9 %fusion.24 = (bf16[16,1,16,128]{3,2,1,0:T(8,128)(2,1)S(1)}, bf16[16,1,16,128]{3,2,1,0:T(8,128)(2,1)S(1)}) fusion(bf16[16,4,16,128]{3,2,1,0:T(8,128)(2,1)} %param.3), kind=kLoop, calls=%fused_computation.61 | loop fusion | bytes 262144 | tf_op jit(solution)/shard_map/slice | solution.py:13
  7.5 4.8 %collective-permute-start = (bf16[16,1,16,128]{3,0,2,1:T(8,128)(2,1)S(1)}, bf16[16,1,16,128]{3,0,2,1:T(8,128)(2,1)S(1)}, u32[]{:S(2)}, u32[]{:S(2)}) collective-permute-start(bf16[16,1,16,128]{3,0,2,1:T(8,128)(2,1)S(1)} %copy.37), channel_id=1, source_target_pairs={{0,16},{16,32},{32,48},{48,64},{64,80},{80,96},{96,112},{112,128},... | collective-permute-start | bytes 196616 | tf_op jit(solution)/shard_map/ppermute | solution.py:14
  12.3 1.3 %collective-permute-start.1 = (bf16[16,1,16,128]{3,0,2,1:T(8,128)(2,1)S(1)}, bf16[16,1,16,128]{3,0,2,1:T(8,128)(2,1)S(1)}, u32[]{:S(2)}, u32[]{:S(2)}) collective-permute-start(bf16[16,1,16,128]{3,0,2,1:T(8,128)(2,1)S(1)} %copy.38), channel_id=1, source_target_pairs={{16,0},{32,16},{48,32},{64,48},{80,64},{96,80},{112,96},{128,112},... | collective-permute-start | bytes 196616 | tf_op jit(solution)/shard_map/ppermute | solution.py:15
  13.6 0.0 collective-permute-done
  13.6 1.1 %constant_dynamic-update-slice_fusion.1 = bf16[16,6,16,128]{3,0,2,1:T(8,128)(2,1)S(1)} fusion(bf16[16,6,16,128]{3,0,2,1:T(8,128)(2,1)S(1)} %constant_dynamic-update-slice_fusion.2, bf16[16,4,16,128]{3,2,1,0:T(8,128)(2,1)} %param.3), kind=kLoop, calls=%fused_computation.58 | loop fusion | bytes 524288
  14.8 3.2 %collective-permute-done.1 = bf16[16,1,16,128]{3,0,2,1:T(8,128)(2,1)S(1)} collective-permute-done((bf16[16,1,16,128]{3,0,2,1:T(8,128)(2,1)S(1)}, bf16[16,1,16,128]{3,0,2,1:T(8,128)(2,1)S(1)}, u32[]{:S(2)}, u32[]{:S(2)}) %collective-permute-start.1) | collective-permute-done | bytes 65568 | tf_op jit(solution)/shard_map/ppermute | solution.py:15
  18.0 3.2 %collective-permute-start.2 = (bf16[16,6,1,128]{3,0,2,1:T(8,128)(2,1)S(1)}, bf16[16,6,1,128]{3,0,2,1:T(8,128)(2,1)S(1)}, u32[]{:S(2)}, u32[]{:S(2)}) collective-permute-start(bf16[16,6,1,128]{3,0,2,1:T(8,128)(2,1)S(1)} %get-tuple-element.5), channel_id=1, source_target_pairs={{0,8},{1,9},{2,10},{3,11},{4,12},{5,13},{6,14},{7,15},{16,24},{17,... | collective-permute-start | bytes 73736 | tf_op jit(solution)/shard_map/ppermute | solution.py:14
  21.2 1.3 %collective-permute-start.3 = (bf16[16,6,1,128]{3,0,2,1:T(8,128)(2,1)S(1)}, bf16[16,6,1,128]{3,0,2,1:T(8,128)(2,1)S(1)}, u32[]{:S(2)}, u32[]{:S(2)}) collective-permute-start(bf16[16,6,1,128]{3,0,2,1:T(8,128)(2,1)S(1)} %get-tuple-element.6), channel_id=1, source_target_pairs={{8,0},{9,1},{10,2},{11,3},{12,4},{13,5},{14,6},{15,7},{24,16},{25,... | collective-permute-start | bytes 73736 | tf_op jit(solution)/shard_map/ppermute | solution.py:15
  22.5 0.0 collective-permute-done.2
  22.5 3.3 %collective-permute-done.3 = bf16[16,6,1,128]{3,0,2,1:T(8,128)(2,1)S(1)} collective-permute-done((bf16[16,6,1,128]{3,0,2,1:T(8,128)(2,1)S(1)}, bf16[16,6,1,128]{3,0,2,1:T(8,128)(2,1)S(1)}, u32[]{:S(2)}, u32[]{:S(2)}) %collective-permute-start.3) | collective-permute-done | bytes 24608 | tf_op jit(solution)/shard_map/ppermute | solution.py:15
  25.8 0.8 pad_maximum_fusion
  26.6 0.0 all-gather.2.cloned.1.call-update
  26.7 0.0 copy-start.1
  26.7 45.2 %all-gather.2.cloned.1.call-done = bf16[128,6,18,128]{3,0,2,1:T(8,128)(2,1)} async-done(((bf16[16,6,18,128]{3,0,2,1:T(8,128)(2,1)}), bf16[128,6,18,128]{3,0,2,1:T(8,128)(2,1)}) %all-gather.2.cloned.1.call-update) | async-done | bytes 3538960 | tf_op jit(solution)/shard_map/all_gather | solution.py:55
  71.9 0.0 copy-start
  71.9 2.7 %convolution_bitcast_fusion = f32[3,3,16,4,18,128]{5,2,4,3,1,0:T(8,128)S(1)} fusion(bf16[128,6,18,128]{3,0,2,1:T(8,128)(2,1)} %all-gather.2.cloned.1.call-done, bf16[3,3,3,16,128]{4,3,2,1,0:T(8,128)(2,1)} %param.4), kind=kOutput, calls=%fused_computation | convolution fusion | flops 339738624 | bytes 7704576 | tf_op jit(solution)/shard_map/dot_general | solution.py:33
  74.6 0.0 copy-done.1
  74.6 0.1 copy-done
  74.6 0.8 convolution_bitcast_fusion.1
  75.5 0.8 convolution_bitcast_fusion.2
  76.3 0.0 copy-start.2
  76.3 0.3 fusion.2
  76.7 0.3 fusion.8
  77.0 0.2 slice.191
  77.2 0.0 copy-done.2
  77.2 0.4 fusion
  77.6 0.8 copy.21
  (5 shorter events, 0.1 us)
Async XLA Ops:
  6.5 65.4 %all-gather.2.cloned.1.call-start = ((), (), s32[]{:S(2)}) async-start(), calls=%async_computation | async-start | bytes 3981312 | tf_op jit(solution)/shard_map/all_gather | solution.py:55
  7.5 6.2 %collective-permute-start = (bf16[16,1,16,128]{3,0,2,1:T(8,128)(2,1)S(1)}, bf16[16,1,16,128]{3,0,2,1:T(8,128)(2,1)S(1)}, u32[]{:S(2)}, u32[]{:S(2)}) collective-permute-start(bf16[16,1,16,128]{3,0,2,1:T(8,128)(2,1)S(1)} %copy.37), channel_id=1, source_target_pairs={{0,16},{16,32},{32,48},{48,64},{64,80},{80,96},{96,112},{112,128},... | collective-permute-start | bytes 196616 | tf_op jit(solution)/shard_map/ppermute | solution.py:14
  12.3 5.6 %collective-permute-start.1 = (bf16[16,1,16,128]{3,0,2,1:T(8,128)(2,1)S(1)}, bf16[16,1,16,128]{3,0,2,1:T(8,128)(2,1)S(1)}, u32[]{:S(2)}, u32[]{:S(2)}) collective-permute-start(bf16[16,1,16,128]{3,0,2,1:T(8,128)(2,1)S(1)} %copy.38), channel_id=1, source_target_pairs={{16,0},{32,16},{48,32},{64,48},{80,64},{96,80},{112,96},{128,112},... | collective-permute-start | bytes 196616 | tf_op jit(solution)/shard_map/ppermute | solution.py:15
  18.0 4.5 %collective-permute-start.2 = (bf16[16,6,1,128]{3,0,2,1:T(8,128)(2,1)S(1)}, bf16[16,6,1,128]{3,0,2,1:T(8,128)(2,1)S(1)}, u32[]{:S(2)}, u32[]{:S(2)}) collective-permute-start(bf16[16,6,1,128]{3,0,2,1:T(8,128)(2,1)S(1)} %get-tuple-element.5), channel_id=1, source_target_pairs={{0,8},{1,9},{2,10},{3,11},{4,12},{5,13},{6,14},{7,15},{16,24},{17,... | collective-permute-start | bytes 73736 | tf_op jit(solution)/shard_map/ppermute | solution.py:14
  21.2 4.6 %collective-permute-start.3 = (bf16[16,6,1,128]{3,0,2,1:T(8,128)(2,1)S(1)}, bf16[16,6,1,128]{3,0,2,1:T(8,128)(2,1)S(1)}, u32[]{:S(2)}, u32[]{:S(2)}) collective-permute-start(bf16[16,6,1,128]{3,0,2,1:T(8,128)(2,1)S(1)} %get-tuple-element.6), channel_id=1, source_target_pairs={{8,0},{9,1},{10,2},{11,3},{12,4},{13,5},{14,6},{15,7},{24,16},{25,... | collective-permute-start | bytes 73736 | tf_op jit(solution)/shard_map/ppermute | solution.py:15
  26.7 47.9 %copy-start.1 = (bf16[3,3,3,16,128]{4,3,2,1,0:T(8,128)(2,1)S(1)}, bf16[3,3,3,16,128]{4,3,2,1,0:T(8,128)(2,1)}, u32[]{:S(2)}) copy-start(bf16[3,3,3,16,128]{4,3,2,1,0:T(8,128)(2,1)} %param.4) | copy-start | bytes 331780
  71.9 2.7 %copy-start = (bf16[128,6,18,128]{3,0,2,1:T(8,128)(2,1)S(1)}, bf16[128,6,18,128]{3,0,2,1:T(8,128)(2,1)}, u32[]{:S(2)}) copy-start(bf16[128,6,18,128]{3,0,2,1:T(8,128)(2,1)} %all-gather.2.cloned.1.call-done) | copy-start | bytes 10616836
  76.3 0.8 copy-start.2
Sparse Core Ops, SparseCore 0:
  26.8 45.0 all-gather.1
where the time goes:
time: 85.4 us; the launch traced here: 85.2 us
  waiting for transfers between devices  51.7 us (61%)
  between operations  13.5 us (16%)
  starting transfers between devices  10.6 us (12%)
  matrix products  4.34 us (5%)
  local copies, waits for them, and re-layouts  3.13 us (4%)
  other arithmetic  1.86 us (2%)
    all_gather x1, waiting for transfers between devices, per_device(): gathered = lax.all_gather(padded, 'col', axis=0, tiled=True)  45.2 us
    ppermute x2, starting transfers between devices, with_halo(): before = lax.ppermute(last, axis, up)  8.02 us
    ppermute x2, waiting for transfers between devices, with_halo(): after = lax.ppermute(first, axis, down)  6.47 us
    dot_general x3, matrix products, convolve(): lax.dot_general(weights[depth_tap], planes, (((3,), (0,)), ((), ())), pre...  4.34 us
    ppermute x2, starting transfers between devices, with_halo(): after = lax.ppermute(first, axis, down)  2.58 us
  transfers between devices with their start and end apart: 5, of which 3 were waited for; matrix products, arithmetic and copies ran while one was open for 1% of the time, Pallas kernels for 0%

commit v1 on v0

--- a/solution.py
+++ b/solution.py
@@ -52,7 +52,9 @@
 
 def per_device(features, kernel, channel_bias):
     padded = with_halo(features, (("dev", 1), ("ha", 2)), 1)
-    gathered = lax.all_gather(padded, "col", axis=0, tiled=True)
+    gathered = jnp.concatenate(
+        lax.all_to_all(jnp.stack([padded] * lax.axis_size("col")), "col", 0, 0), axis=0
+    )
     return finish(convolve(gathered, kernel), channel_bias)
 
 

time: 85.4 us -> 80.2 us (0.939)
  the two profiles are of different devices: /device:TPU:1 before, /device:TPU:48 now
where the time goes in v1:
time: 80.2 us; the launch traced here: 79.9 us
  blocking collectives  46.8 us (58%)
  starting transfers between devices  17.9 us (22%)
  waiting for transfers between devices  6.42 us (8%)
  local copies, waits for them, and re-layouts  4.82 us (6%)
  matrix products  2.51 us (3%)
  other arithmetic  1.37 us (2%)
    all_to_all x1, blocking collectives, per_device(): lax.all_to_all(jnp.stack([padded] * lax.axis_size('col')), 'col', 0, 0)  46.8 us
    ppermute x2, starting transfers between devices, with_halo(): after = lax.ppermute(first, axis, down)  11.5 us
    ppermute x2, starting transfers between devices, with_halo(): before = lax.ppermute(last, axis, up)  6.44 us
    ppermute x2, waiting for transfers between devices, with_halo(): after = lax.ppermute(first, axis, down)  4.43 us
    dot_general x3, matrix products, convolve(): lax.dot_general(weights[depth_tap], planes, (((3,), (0,)), ((), ())), pre...  2.51 us
    ppermute x2, waiting for transfers between devices, with_halo(): before = lax.ppermute(last, axis, up)  1.99 us
  transfers between devices with their start and end apart: 4, of which 4 were waited for; matrix products, arithmetic and copies ran while one was open for 1% of the time, Pallas kernels for 0%

profile of v1, /device:TPU:48, one launch (start us, length us, event | category | flops | bytes accessed | tf_op | source)
XLA Modules:
  0.0 79.9 jit_solution(2465866957395272365)
XLA Ops:
  0.0 0.9 %fusion.24 = (bf16[16,1,16,128]{3,2,1,0:T(8,128)(2,1)S(1)}, bf16[16,1,16,128]{3,2,1,0:T(8,128)(2,1)S(1)}) fusion(bf16[16,4,16,128]{3,2,1,0:T(8,128)(2,1)} %param.3), kind=kLoop, calls=%fused_computation.61 | loop fusion | bytes 262144 | tf_op jit(solution)/shard_map/slice | solution.py:13
  0.9 4.3 %collective-permute-start = (bf16[16,1,16,128]{3,2,1,0:T(8,128)(2,1)S(1)}, bf16[16,1,16,128]{3,2,1,0:T(8,128)(2,1)S(1)}, u32[]{:S(2)}, u32[]{:S(2)}) collective-permute-start(bf16[16,1,16,128]{3,2,1,0:T(8,128)(2,1)S(1)} %get-tuple-element.8), channel_id=1, source_target_pairs={{0,16},{16,32},{32,48},{48,64},{64,80},{80,96},{96,112},{112,128},... | collective-permute-start | bytes 196616 | tf_op jit(solution)/shard_map/ppermute | solution.py:14
  5.2 10.2 %collective-permute-start.1 = (bf16[16,1,16,128]{3,2,1,0:T(8,128)(2,1)S(1)}, bf16[16,1,16,128]{3,2,1,0:T(8,128)(2,1)S(1)}, u32[]{:S(2)}, u32[]{:S(2)}) collective-permute-start(bf16[16,1,16,128]{3,2,1,0:T(8,128)(2,1)S(1)} %get-tuple-element.7), channel_id=1, source_target_pairs={{16,0},{32,16},{48,32},{64,48},{80,64},{96,80},{112,96},{128,112},... | collective-permute-start | bytes 196616 | tf_op jit(solution)/shard_map/ppermute | solution.py:15
  15.3 1.6 %collective-permute-done = bf16[16,1,16,128]{3,2,1,0:T(8,128)(2,1)S(1)} collective-permute-done((bf16[16,1,16,128]{3,2,1,0:T(8,128)(2,1)S(1)}, bf16[16,1,16,128]{3,2,1,0:T(8,128)(2,1)S(1)}, u32[]{:S(2)}, u32[]{:S(2)}) %collective-permute-start) | collective-permute-done | bytes 65568 | tf_op jit(solution)/shard_map/ppermute | solution.py:14
  16.9 1.0 %constant_dynamic-update-slice_fusion.1 = bf16[16,6,16,128]{3,2,1,0:T(8,128)(2,1)S(1)} fusion(bf16[16,6,16,128]{3,2,1,0:T(8,128)(2,1)S(1)} %constant_dynamic-update-slice_fusion.2, bf16[16,4,16,128]{3,2,1,0:T(8,128)(2,1)} %param.3), kind=kLoop, calls=%fused_computation.58 | loop fusion | bytes 524288
  17.9 0.2 collective-permute-done.1
  18.1 0.1 fusion.23
  18.2 2.2 %collective-permute-start.2 = (bf16[16,6,1,128]{3,2,1,0:T(2,128)(2,1)S(1)}, bf16[16,6,1,128]{3,2,1,0:T(2,128)(2,1)S(1)}, u32[]{:S(2)}, u32[]{:S(2)}) collective-permute-start(bf16[16,6,1,128]{3,2,1,0:T(2,128)(2,1)S(1)} %get-tuple-element.5), channel_id=1, source_target_pairs={{0,8},{1,9},{2,10},{3,11},{4,12},{5,13},{6,14},{7,15},{16,24},{17,... | collective-permute-start | bytes 73736 | tf_op jit(solution)/shard_map/ppermute | solution.py:14
  20.3 1.3 %collective-permute-start.3 = (bf16[16,6,1,128]{3,2,1,0:T(2,128)(2,1)S(1)}, bf16[16,6,1,128]{3,2,1,0:T(2,128)(2,1)S(1)}, u32[]{:S(2)}, u32[]{:S(2)}) collective-permute-start(bf16[16,6,1,128]{3,2,1,0:T(2,128)(2,1)S(1)} %get-tuple-element.6), channel_id=1, source_target_pairs={{8,0},{9,1},{10,2},{11,3},{12,4},{13,5},{14,6},{15,7},{24,16},{25,... | collective-permute-start | bytes 73736 | tf_op jit(solution)/shard_map/ppermute | solution.py:15
  21.6 0.4 collective-permute-done.2
  22.1 4.3 %collective-permute-done.3 = bf16[16,6,1,128]{3,2,1,0:T(2,128)(2,1)S(1)} collective-permute-done((bf16[16,6,1,128]{3,2,1,0:T(2,128)(2,1)S(1)}, bf16[16,6,1,128]{3,2,1,0:T(2,128)(2,1)S(1)}, u32[]{:S(2)}, u32[]{:S(2)}) %collective-permute-start.3) | collective-permute-done | bytes 24608 | tf_op jit(solution)/shard_map/ppermute | solution.py:15
  26.3 0.3 pad_maximum_fusion
  26.7 0.1 copy.20
  26.8 0.6 stack.2
  27.4 46.8 %all_to_all.5 = bf16[8,16,6,18,128]{4,1,3,2,0:T(8,128)(2,1)S(1)} all-to-all(bf16[8,16,6,18,128]{4,1,3,2,0:T(8,128)(2,1)S(1)} %stack.2), channel_id=1, replica_groups=mesh['dev'=32,'ha'=2,'col'=8] {'col'}, dimensions={0} | all-to-all | bytes 7077888 | tf_op jit(solution)/shard_map/all_to_all | solution.py:56
  74.1 0.0 copy-start
  74.1 1.0 %copy.21 = bf16[8,16,6,18,128]{4,1,0,3,2:T(8,128)(2,1)S(1)} copy(bf16[8,16,6,18,128]{4,1,3,2,0:T(8,128)(2,1)S(1)} %all_to_all.5) | data formatting | bytes 7077888 | tf_op jit(solution)/shard_map/all_to_all | solution.py:56
  75.2 0.0 copy-done
  75.2 0.8 %convolution_bitcast_fusion = f32[3,3,16,4,18,128]{5,2,4,3,1,0:T(8,128)S(1)} fusion(bf16[128,6,18,128]{3,0,2,1:T(8,128)(2,1)S(1)} %bitcast.126, bf16[3,3,3,16,128]{4,3,2,1,0:T(8,128)(2,1)S(1)} %copy-done), kind=kOutput, calls=%fused_computation | convolution fusion | flops 339738624 | bytes 7704576 | tf_op jit(solution)/shard_map/dot_general | solution.py:33
  76.0 0.8 %convolution_bitcast_fusion.1 = f32[3,3,16,4,18,128]{5,2,4,3,1,0:T(8,128)S(1)} fusion(bf16[128,6,18,128]{3,0,2,1:T(8,128)(2,1)S(1)} %bitcast.127, bf16[3,3,3,16,128]{4,3,2,1,0:T(8,128)(2,1)S(1)} %copy-done), kind=kOutput, calls=%fused_computation.1 | convolution fusion | flops 339738624 | bytes 7704576 | tf_op jit(solution)/shard_map/dot_general | solution.py:33
  76.9 0.8 %convolution_bitcast_fusion.2 = f32[3,3,16,4,18,128]{5,2,1,0,4,3:T(8,128)S(1)} fusion(bf16[128,6,18,128]{3,0,2,1:T(8,128)(2,1)S(1)} %bitcast.128, bf16[3,3,3,16,128]{4,3,2,1,0:T(8,128)(2,1)S(1)} %copy-done), kind=kOutput, calls=%fused_computation.2 | convolution fusion | flops 339738624 | bytes 7704576 | tf_op jit(solution)/shard_map/dot_general | solution.py:33
  77.7 0.3 fusion.2
  78.1 0.0 copy-start.1
  78.1 0.3 fusion.8
  78.4 0.2 slice.189
  78.6 0.1 copy-done.1
  78.7 0.4 fusion
  79.1 0.8 copy.36
  (2 shorter events, 0.0 us)
Async XLA Ops:
  0.9 16.0 %collective-permute-start = (bf16[16,1,16,128]{3,2,1,0:T(8,128)(2,1)S(1)}, bf16[16,1,16,128]{3,2,1,0:T(8,128)(2,1)S(1)}, u32[]{:S(2)}, u32[]{:S(2)}) collective-permute-start(bf16[16,1,16,128]{3,2,1,0:T(8,128)(2,1)S(1)} %get-tuple-element.8), channel_id=1, source_target_pairs={{0,16},{16,32},{32,48},{48,64},{64,80},{80,96},{96,112},{112,128},... | collective-permute-start | bytes 196616 | tf_op jit(solution)/shard_map/ppermute | solution.py:14
  5.2 12.9 %collective-permute-start.1 = (bf16[16,1,16,128]{3,2,1,0:T(8,128)(2,1)S(1)}, bf16[16,1,16,128]{3,2,1,0:T(8,128)(2,1)S(1)}, u32[]{:S(2)}, u32[]{:S(2)}) collective-permute-start(bf16[16,1,16,128]{3,2,1,0:T(8,128)(2,1)S(1)} %get-tuple-element.7), channel_id=1, source_target_pairs={{16,0},{32,16},{48,32},{64,48},{80,64},{96,80},{112,96},{128,112},... | collective-permute-start | bytes 196616 | tf_op jit(solution)/shard_map/ppermute | solution.py:15
  18.2 3.9 %collective-permute-start.2 = (bf16[16,6,1,128]{3,2,1,0:T(2,128)(2,1)S(1)}, bf16[16,6,1,128]{3,2,1,0:T(2,128)(2,1)S(1)}, u32[]{:S(2)}, u32[]{:S(2)}) collective-permute-start(bf16[16,6,1,128]{3,2,1,0:T(2,128)(2,1)S(1)} %get-tuple-element.5), channel_id=1, source_target_pairs={{0,8},{1,9},{2,10},{3,11},{4,12},{5,13},{6,14},{7,15},{16,24},{17,... | collective-permute-start | bytes 73736 | tf_op jit(solution)/shard_map/ppermute | solution.py:14
  20.3 6.0 %collective-permute-start.3 = (bf16[16,6,1,128]{3,2,1,0:T(2,128)(2,1)S(1)}, bf16[16,6,1,128]{3,2,1,0:T(2,128)(2,1)S(1)}, u32[]{:S(2)}, u32[]{:S(2)}) collective-permute-start(bf16[16,6,1,128]{3,2,1,0:T(2,128)(2,1)S(1)} %get-tuple-element.6), channel_id=1, source_target_pairs={{8,0},{9,1},{10,2},{11,3},{12,4},{13,5},{14,6},{15,7},{24,16},{25,... | collective-permute-start | bytes 73736 | tf_op jit(solution)/shard_map/ppermute | solution.py:15
  74.1 1.1 %copy-start = (bf16[3,3,3,16,128]{4,3,2,1,0:T(8,128)(2,1)S(1)}, bf16[3,3,3,16,128]{4,3,2,1,0:T(8,128)(2,1)}, u32[]{:S(2)}) copy-start(bf16[3,3,3,16,128]{4,3,2,1,0:T(8,128)(2,1)} %param.4) | copy-start | bytes 331780
  78.1 0.7 copy-start.1
